TPU v7x, 512 devices: a whole 4x4x16 slice. The times are simulated.
512 devices in a mesh: dp: 8 (over y, core), station: 64 (over x, z).
Axes of the slice: x: 4, y: 4, z: 16, core: 2. Of those that a mesh axis runs over, the one named last changes fastest.
Arguments:
- query_states: bfloat16 [8, 64, 128, 768], P('dp', 'station'), may hold values from -6 to 6
- key_states: bfloat16 [8, 64, 128, 768], P('dp', 'station'), may hold values from -6 to 6
- value_states: bfloat16 [8, 64, 128, 768], P('dp', 'station'), may hold values from -15 to 15
- grad_output: bfloat16 [8, 64, 128, 768], P('dp', 'station'), may hold values from -6 to 6
- out_weight: bfloat16 [768, 768], replicated, may hold values from -0.21875 to 0.21875
- partner_ids: int32 [64, 6], replicated, may hold values from 0 to 63, as said below
- partner_count: int32 [64], replicated, may hold values from 1 to 6, as said below
Outputs:
- layer_output: bfloat16 [8, 64, 128, 768], P('dp', 'station')
- grad_query: bfloat16 [8, 64, 128, 768], P('dp', 'station')
- grad_key: bfloat16 [8, 64, 128, 768], P('dp', 'station')
- grad_value: bfloat16 [8, 64, 128, 768], P('dp', 'station')
- grad_weight: float32 [768, 768], P('dp')
Inputs may be any that keep to these rules, and one draw needn't show every extreme that they name: `partner_ids`: row s lists 6 different stations other than s, all held by devices within 3 places of the device of s along the station axis, taken as a loop (station s lies on device s); only the first partner_count[s] entries are partners. `partner_count`: some station has exactly 6 partners.
All inputs are finite; a program needn't handle non-finite values.
Results may differ from a plain program's by a relative error of at most 0.025.
Values may be sent and summed in bfloat16 or wider, within the bound.
A program may use at most 64 MiB of HBM per device.

v0:
```python
import math

import jax
import jax.numpy as jnp
from jax import lax
from jax.sharding import PartitionSpec as P

HEADS = 12
PMAX = 6
HOPS = 3


neg_big = -1e30


def from_behind(value, axis, steps):
    count = lax.axis_size(axis)
    pairs = [(source, (source + steps) % count) for source in range(count)]
    return lax.ppermute(value, axis, pairs)


def split_heads(rows_in, head_count):
    return rows_in.reshape(rows_in.shape[:-1] + (head_count, rows_in.shape[-1] // head_count))


def local(
    query_states, key_states, value_states, grad_output, out_weight, partner_ids, partner_count
):
    window_count, per_device, span_rows, model_width = query_states.shape
    head_count = HEADS
    head_width = model_width // head_count
    score_scale = 1.0 / math.sqrt(head_width)
    slot_count = PMAX + 1
    device_count = lax.axis_size("station")
    station_count = per_device * device_count
    device_no = lax.axis_index("station")
    candidates = (2 * HOPS + 1) * per_device
    first_station = (device_no - HOPS) * per_device
    key_value = jnp.stack([key_states, value_states], 0)
    pieces = []
    for offset in range(-HOPS, HOPS + 1):
        if offset == 0:
            pieces.append(key_value)
        else:
            pieces.append(from_behind(key_value, "station", -offset))
    window = jnp.concatenate(pieces, 2)
    my_partners = lax.dynamic_slice_in_dim(partner_ids, device_no * per_device, per_device, 0)
    my_counts = lax.dynamic_slice_in_dim(partner_count, device_no * per_device, per_device, 0)
    partner_pos = jnp.mod(my_partners - first_station, station_count)
    self_pos = HOPS * per_device + jnp.arange(per_device, dtype=jnp.int32)
    slot_station = jnp.concatenate([self_pos[:, None], partner_pos], 1)
    slot_live = jnp.arange(slot_count, dtype=jnp.int32)[None, :] <= my_counts[:, None]
    row_count = window_count * per_device * span_rows
    flat_grad = grad_output.reshape(row_count, model_width)
    grad_mixed = lax.dot_general(
        flat_grad, out_weight, (((1,), (1,)), ((), ())), preferred_element_type=jnp.float32
    ).astype(jnp.bfloat16)
    grad_mixed = grad_mixed.reshape(query_states.shape)

    def one_station(number):
        window_no = number // per_device
        station_no = number % per_device
        query_rows = split_heads(query_states[window_no, station_no], head_count)
        grad_rows = split_heads(grad_mixed[window_no, station_no], head_count)
        picked = jnp.take(window[:, window_no], slot_station[station_no], axis=1)
        key_rows = picked[0].reshape(slot_count * span_rows, head_count, head_width)
        value_rows = picked[1].reshape(slot_count * span_rows, head_count, head_width)
        allowed = jnp.repeat(slot_live[station_no].astype(jnp.float32), span_rows)
        scores = (
            jnp.einsum("qhd,khd->hqk", query_rows, key_rows, preferred_element_type=jnp.float32)
            * score_scale
        )
        masked = jnp.where(allowed[None, None, :] > 0, scores, neg_big)
        row_max = jnp.max(masked, -1)
        weights_raw = jnp.exp(masked - row_max[..., None])
        row_sum = jnp.sum(weights_raw, -1)
        attn_probs = weights_raw / row_sum[..., None]
        probs_half = attn_probs.astype(jnp.bfloat16)
        mixed_rows = jnp.einsum(
            "hqk,khd->qhd", probs_half, value_rows, preferred_element_type=jnp.float32
        ).astype(jnp.bfloat16)
        row_delta = jnp.sum(grad_rows.astype(jnp.float32) * mixed_rows.astype(jnp.float32), -1).T
        grad_probs = jnp.einsum(
            "qhd,khd->hqk", grad_rows, value_rows, preferred_element_type=jnp.float32
        )
        grad_scores = (attn_probs * (grad_probs - row_delta[..., None])).astype(jnp.bfloat16)
        query_grad = (
            score_scale
            * jnp.einsum("hqk,khd->qhd", grad_scores, key_rows, preferred_element_type=jnp.float32)
        ).astype(jnp.bfloat16)
        result = (
            mixed_rows.reshape(span_rows, model_width),
            query_grad.reshape(span_rows, model_width),
        )
        key_part = score_scale * jnp.einsum(
            "hqk,qhd->khd", grad_scores, query_rows, preferred_element_type=jnp.float32
        )
        value_part = jnp.einsum(
            "hqk,qhd->khd", probs_half, grad_rows, preferred_element_type=jnp.float32
        )
        result = result + (
            jnp.stack([key_part, value_part], 0).reshape(2, -1, span_rows, model_width),
        )
        return result

    outputs = lax.map(one_station, jnp.arange(window_count * per_device, dtype=jnp.int32))
    mixed_all = outputs[0].reshape(query_states.shape)
    grad_query = outputs[1].reshape(query_states.shape)
    contribution = outputs[2].reshape(window_count, per_device, 2, -1, span_rows, model_width)
    moved = jnp.moveaxis(contribution, 2, 0).reshape(
        2, window_count, per_device * slot_count, span_rows, model_width
    )
    flat_slots = slot_station.reshape(-1)
    spread = (
        jnp.zeros((2, window_count, candidates, span_rows, model_width), jnp.float32)
        .at[:, :, flat_slots]
        .add(moved)
    )
    own_grads = spread[:, :, HOPS * per_device : (HOPS + 1) * per_device]
    for offset in range(-HOPS, HOPS + 1):
        if offset != 0:
            lower = (offset + HOPS) * per_device
            own_grads = own_grads + from_behind(
                spread[:, :, lower : lower + per_device].astype(jnp.bfloat16), "station", offset
            ).astype(jnp.float32)
    mixed_flat = mixed_all.reshape(row_count, model_width)
    layer_output = jnp.dot(mixed_flat, out_weight, preferred_element_type=jnp.float32).astype(
        jnp.bfloat16
    )
    grad_weight = lax.psum_scatter(
        lax.dot_general(
            mixed_flat, flat_grad, (((0,), (0,)), ((), ())), preferred_element_type=jnp.float32
        ).astype(jnp.bfloat16),
        "dp",
        scatter_dimension=0,
        tiled=True,
    ).astype(jnp.float32)
    grad_weight = lax.psum(grad_weight, "station")
    grad_weight = grad_weight / math.sqrt(row_count * lax.axis_size("dp") * device_count)
    return (
        layer_output.reshape(query_states.shape),
        grad_query,
        own_grads[0].astype(jnp.bfloat16),
        own_grads[1].astype(jnp.bfloat16),
        grad_weight,
    )


def solution(mesh):
    return jax.shard_map(
        local,
        mesh=mesh,
        in_specs=(
            P("dp", "station", None, None),
            P("dp", "station", None, None),
            P("dp", "station", None, None),
            P("dp", "station", None, None),
            P(),
            P(),
            P(),
        ),
        out_specs=(
            P("dp", "station", None, None),
            P("dp", "station", None, None),
            P("dp", "station", None, None),
            P("dp", "station", None, None),
            P("dp", None),
        ),
        check_vma=False,
    )
```

profile of v0, /device:TPU:24, one launch (start us, length us, event | category | flops | bytes accessed | tf_op | source)
XLA Modules:
  0.0 522.0 jit_solution(13839279402721123467)
XLA Ops:
  7.3 1.2 pad_maximum_fusion
  8.4 6.5 %collective-permute-start = (bf16[2,1,1,128,768]{4,3,2,1,0:T(8,128)(2,1)S(1)}, bf16[2,1,1,128,768]{4,3,2,1,0:T(8,128)(2,1)}, u32[]{:S(2)}, u32[]{:S(2)}) collective-permute-start(bf16[2,1,1,128,768]{4,3,2,1,0:T(8,128)(2,1)S(1)} %pad_maximum_fusion), channel_id=1, source_target_pairs={{0,3},{1,4},{2,5},{3,6},{4,7},{5,8},{6,9},{7,10},{8,11},{9,12},{10... | collective-permute-start | bytes 1179656 | tf_op jit(solution)/shard_map/ppermute | solution.py:19
  15.0 6.4 %collective-permute-start.1 = (bf16[2,1,1,128,768]{4,3,2,1,0:T(8,128)(2,1)S(1)}, bf16[2,1,1,128,768]{4,3,2,1,0:T(8,128)(2,1)}, u32[]{:S(2)}, u32[]{:S(2)}) collective-permute-start(bf16[2,1,1,128,768]{4,3,2,1,0:T(8,128)(2,1)S(1)} %pad_maximum_fusion), channel_id=1, source_target_pairs={{0,2},{1,3},{2,4},{3,5},{4,6},{5,7},{6,8},{7,9},{8,10},{9,11},{10,... | collective-permute-start | bytes 1179656 | tf_op jit(solution)/shard_map/ppermute | solution.py:19
  21.4 3.8 collective-permute-start.2
  25.2 5.3 %collective-permute-start.3 = (bf16[2,1,1,128,768]{4,3,2,1,0:T(8,128)(2,1)S(1)}, bf16[2,1,1,128,768]{4,3,2,1,0:T(8,128)(2,1)S(1)}, u32[]{:S(2)}, u32[]{:S(2)}) collective-permute-start(bf16[2,1,1,128,768]{4,3,2,1,0:T(8,128)(2,1)S(1)} %pad_maximum_fusion), channel_id=1, source_target_pairs={{0,63},{1,0},{2,1},{3,2},{4,3},{5,4},{6,5},{7,6},{8,7},{9,8},{10,9... | collective-permute-start | bytes 1179656 | tf_op jit(solution)/shard_map/ppermute | solution.py:19
  30.6 2.1 collective-permute-start.4
  32.7 1.2 dynamic_slice.20
  33.9 0.7 fusion.22
  34.6 1.5 convolution_convert_fusion.2
  36.1 0.8 add_select_fusion
  36.9 0.1 add_reduce_fusion
  37.0 0.2 copy.39
  37.2 0.2 copy.37
  37.4 11.0 %collective-permute-done = bf16[2,1,1,128,768]{4,3,2,1,0:T(8,128)(2,1)} collective-permute-done((bf16[2,1,1,128,768]{4,3,2,1,0:T(8,128)(2,1)S(1)}, bf16[2,1,1,128,768]{4,3,2,1,0:T(8,128)(2,1)}, u32[]{:S(2)}, u32[]{:S(2)}) %collective-permute-start) | collective-permute-done | bytes 393248 | tf_op jit(solution)/shard_map/ppermute | solution.py:19
  48.4 5.5 %collective-permute-start.5 = (bf16[2,1,1,128,768]{4,3,2,1,0:T(8,128)(2,1)S(1)}, bf16[2,1,1,128,768]{4,3,2,1,0:T(8,128)(2,1)S(1)}, u32[]{:S(2)}, u32[]{:S(2)}) collective-permute-start(bf16[2,1,1,128,768]{4,3,2,1,0:T(8,128)(2,1)S(1)} %pad_maximum_fusion), channel_id=1, source_target_pairs={{0,61},{1,62},{2,63},{3,0},{4,1},{5,2},{6,3},{7,4},{8,5},{9,6},{10... | collective-permute-start | bytes 1179656 | tf_op jit(solution)/shard_map/ppermute | solution.py:19
  53.9 1.8 constant_dynamic-update-slice_fusion.6
  55.7 8.0 %collective-permute-done.1 = bf16[2,1,1,128,768]{4,3,2,1,0:T(8,128)(2,1)} collective-permute-done((bf16[2,1,1,128,768]{4,3,2,1,0:T(8,128)(2,1)S(1)}, bf16[2,1,1,128,768]{4,3,2,1,0:T(8,128)(2,1)}, u32[]{:S(2)}, u32[]{:S(2)}) %collective-permute-start.1) | collective-permute-done | bytes 393248 | tf_op jit(solution)/shard_map/ppermute | solution.py:19
  63.7 1.8 constant_dynamic-update-slice_fusion.5
  65.5 8.0 %collective-permute-done.2 = bf16[2,1,1,128,768]{4,3,2,1,0:T(8,128)(2,1)} collective-permute-done((bf16[2,1,1,128,768]{4,3,2,1,0:T(8,128)(2,1)S(1)}, bf16[2,1,1,128,768]{4,3,2,1,0:T(8,128)(2,1)}, u32[]{:S(2)}, u32[]{:S(2)}) %collective-permute-start.2) | collective-permute-done | bytes 393248 | tf_op jit(solution)/shard_map/ppermute | solution.py:19
  73.5 1.8 constant_dynamic-update-slice_fusion.4
  75.3 0.8 constant_dynamic-update-slice_fusion.3
  76.1 0.8 constant_dynamic-update-slice_fusion.2
  76.8 0.8 constant_dynamic-update-slice_fusion.1
  77.6 0.9 collective-permute-done.5
  78.5 0.8 constant_dynamic-update-slice_fusion
  79.3 4.1 gather_fusion
  83.4 2.1 select_bitcast_fusion
  85.6 1.7 fusion.27
  87.3 2.1 copy.35
  89.4 2.5 squeeze.36
  91.9 2.1 copy.36
  94.0 2.5 squeeze.37
  96.5 5.9 %fusion.28 = (f32[12,128]{1,0:T(8,128)S(1)}, f32[12,128,896]{1,2,0:T(8,128)}) fusion(pred[896]{0:T(1024)(128)(4,1)S(1)} %broadcast_bitcast_fusion, bf16[896,12,64]{0,2,1:T(8,128)(2,1)} %squeeze.37, bf16[128,12,64]{0,2,1:T(8,128)(2,1)S(1)} %bitcast.88), kind=kOutput, calls=%fused_computation.65 | convolution fusion | flops 181666688 | bytes 7084928 | tf_op jit(solution)/shard_map/while/body/eval_jaxpr/sub | solution.py:75
  102.4 3.3 fusion.8
  105.7 2.7 convolution_bitcast_fusion
  108.4 0.7 multiply_reduce_fusion
  109.1 2.9 multiply_convert_fusion
  112.0 4.2 stack.25
  116.2 4.5 multiply_bitcast_fusion
  120.7 4.2 stack.24
  124.9 1.5 convolution_convert_fusion
  126.4 6.1 %maximum_bitcast_fusion = f32[7,2,128,768]{2,0,3,1:T(8,128)} fusion(f32[1,1,7,128,768]{3,2,4,1,0:T(8,128)} %stack.25, f32[1,1,7,128,768]{3,2,4,1,0:T(8,128)} %stack.24), kind=kLoop, calls=%fused_computation.3 | loop fusion | flops 1376256 | bytes 11010048 | tf_op jit(solution)/shard_map/while/body/eval_jaxpr/stack | solution.py:102
  132.5 6.4 %copy.44 = f32[7,2,128,768]{3,2,1,0:T(8,128)} copy(f32[7,2,128,768]{2,0,3,1:T(8,128)} %maximum_bitcast_fusion) | data formatting | bytes 11010048 | tf_op jit(solution)/shard_map/while/body/eval_jaxpr/stack | solution.py:102
  138.9 3.0 broadcast.96
  141.8 14.2 %scatter_fusion = f32[2,7,128,768]{3,2,1,0:T(8,128)} fusion(f32[2,7,128,768]{3,2,1,0:T(8,128)} %broadcast.96, s32[7]{0:T(128)S(1)} %fusion.23, f32[7,2,128,768]{3,2,1,0:T(8,128)} %copy.44), kind=kCustom, calls=%fused_computation.1 | custom fusion | flops 1376256 | bytes 16515100 | tf_op jit(solution)/shard_map/scatter-add | solution.py:117
  156.0 2.9 bitcast_convert_fusion
  158.9 1.1 fusion.26
  160.0 2.7 collective-permute-start.11
  162.7 10.5 %collective-permute-start.10 = (bf16[2,1,1,128,768]{4,3,2,0,1:T(8,128)(2,1)}, bf16[2,1,1,128,768]{4,3,2,0,1:T(8,128)(2,1)S(1)}, u32[]{:S(2)}, u32[]{:S(2)}) collective-permute-start(bf16[2,1,1,128,768]{4,3,2,0,1:T(8,128)(2,1)} %get-tuple-element.49), channel_id=1, source_target_pairs={{0,2},{1,3},{2,4},{3,5},{4,6},{5,7},{6,8},{7,9},{8,10},{9,11},{10,... | collective-permute-start | bytes 1179656 | tf_op jit(solution)/shard_map/ppermute | solution.py:19
  173.2 2.3 collective-permute-start.9
  175.5 6.9 %collective-permute-start.8 = (bf16[2,1,1,128,768]{4,3,2,0,1:T(8,128)(2,1)}, bf16[2,1,1,128,768]{4,3,2,0,1:T(8,128)(2,1)}, u32[]{:S(2)}, u32[]{:S(2)}) collective-permute-start(bf16[2,1,1,128,768]{4,3,2,0,1:T(8,128)(2,1)} %get-tuple-element.51), channel_id=1, source_target_pairs={{0,63},{1,0},{2,1},{3,2},{4,3},{5,4},{6,5},{7,6},{8,7},{9,8},{10,9... | collective-permute-start | bytes 1179656 | tf_op jit(solution)/shard_map/ppermute | solution.py:19
  182.4 2.0 collective-permute-start.7
  184.5 11.3 %collective-permute-done.11 = bf16[2,1,1,128,768]{4,3,2,0,1:T(8,128)(2,1)S(1)} collective-permute-done((bf16[2,1,1,128,768]{4,3,2,0,1:T(8,128)(2,1)S(1)}, bf16[2,1,1,128,768]{4,3,2,0,1:T(8,128)(2,1)S(1)}, u32[]{:S(2)}, u32[]{:S(2)}) %collective-permute-start.11) | collective-permute-done | bytes 393248 | tf_op jit(solution)/shard_map/ppermute | solution.py:19
  195.8 1.9 collective-permute-start.6
  197.7 0.7 fusion.9
  198.4 0.8 copy.45
  199.2 1.0 fusion.10
  200.2 9.9 %collective-permute-done.10 = bf16[2,1,1,128,768]{4,3,2,0,1:T(8,128)(2,1)S(1)} collective-permute-done((bf16[2,1,1,128,768]{4,3,2,0,1:T(8,128)(2,1)}, bf16[2,1,1,128,768]{4,3,2,0,1:T(8,128)(2,1)S(1)}, u32[]{:S(2)}, u32[]{:S(2)}) %collective-permute-start.10) | collective-permute-done | bytes 393248 | tf_op jit(solution)/shard_map/ppermute | solution.py:19
  210.2 9.9 %collective-permute-done.9 = bf16[2,1,1,128,768]{4,3,2,0,1:T(8,128)(2,1)S(1)} collective-permute-done((bf16[2,1,1,128,768]{4,3,2,0,1:T(8,128)(2,1)}, bf16[2,1,1,128,768]{4,3,2,0,1:T(8,128)(2,1)S(1)}, u32[]{:S(2)}, u32[]{:S(2)}) %collective-permute-start.9) | collective-permute-done | bytes 393248 | tf_op jit(solution)/shard_map/ppermute | solution.py:19
  220.0 7.8 %collective-permute-done.6 = bf16[2,1,1,128,768]{4,3,2,0,1:T(8,128)(2,1)} collective-permute-done((bf16[2,1,1,128,768]{4,3,2,0,1:T(8,128)(2,1)S(1)}, bf16[2,1,1,128,768]{4,3,2,0,1:T(8,128)(2,1)}, u32[]{:S(2)}, u32[]{:S(2)}) %collective-permute-start.6) | collective-permute-done | bytes 393248 | tf_op jit(solution)/shard_map/ppermute | solution.py:19
  227.9 1.8 fusion.16
  229.7 0.8 slice_bitcast_fusion
  230.4 284.0 %all-reduce.1 = f32[96,768]{1,0:T(8,128)S(1)} all-reduce(bf16[96,768]{1,0:T(8,128)(2,1)} %reduce-scatter.2.cloned.1.call-done), channel_id=1, replica_groups=mesh['dp'=8,'station'=64] {'station'}, use_global_device_ids=true, to_apply=%region_5.6 | all-reduce | flops 73728 | bytes 442368 | tf_op jit(solution)/shard_map/psum | solution.py:138
  514.4 0.7 broadcast_multiply_fusion
  (32 shorter events, 0.2 us)
Async XLA Ops:
  7.2 27.5 %copy-start = (bf16[768,768]{1,0:T(8,128)(2,1)S(1)}, bf16[768,768]{1,0:T(8,128)(2,1)}, u32[]{:S(2)}) copy-start(bf16[768,768]{1,0:T(8,128)(2,1)} %param.11) | copy-start | bytes 3538948
  7.2 30.0 %copy-start.7 = (bf16[1,1,128,768]{3,2,1,0:T(8,128)(2,1)S(1)}, bf16[1,1,128,768]{3,2,1,0:T(8,128)(2,1)}, u32[]{:S(2)}) copy-start(bf16[1,1,128,768]{3,2,1,0:T(8,128)(2,1)} %param.7) | copy-start | bytes 589828
  7.2 223.2 %reduce-scatter.2.cloned.1.call-start = ((), (), s32[]{:S(2)}) async-start(), calls=%async_computation.1 | async-start | bytes 1327104 | tf_op jit(solution)/shard_map/reduce_scatter | solution.py:130
  7.2 68.0 %copy-start.5 = (bf16[1,1,128,768]{3,2,1,0:T(8,128)(2,1)S(1)}, bf16[1,1,128,768]{3,2,1,0:T(8,128)(2,1)}, u32[]{:S(2)}) copy-start(bf16[1,1,128,768]{3,2,1,0:T(8,128)(2,1)} %param.9) | copy-start | bytes 589828
  7.2 68.0 %copy-start.6 = (bf16[1,1,128,768]{3,2,1,0:T(8,128)(2,1)S(1)}, bf16[1,1,128,768]{3,2,1,0:T(8,128)(2,1)}, u32[]{:S(2)}) copy-start(bf16[1,1,128,768]{3,2,1,0:T(8,128)(2,1)} %param.8) | copy-start | bytes 589828
  8.4 40.0 %collective-permute-start = (bf16[2,1,1,128,768]{4,3,2,1,0:T(8,128)(2,1)S(1)}, bf16[2,1,1,128,768]{4,3,2,1,0:T(8,128)(2,1)}, u32[]{:S(2)}, u32[]{:S(2)}) collective-permute-start(bf16[2,1,1,128,768]{4,3,2,1,0:T(8,128)(2,1)S(1)} %pad_maximum_fusion), channel_id=1, source_target_pairs={{0,3},{1,4},{2,5},{3,6},{4,7},{5,8},{6,9},{7,10},{8,11},{9,12},{10... | collective-permute-start | bytes 1179656 | tf_op jit(solution)/shard_map/ppermute | solution.py:19
  15.0 48.7 %collective-permute-start.1 = (bf16[2,1,1,128,768]{4,3,2,1,0:T(8,128)(2,1)S(1)}, bf16[2,1,1,128,768]{4,3,2,1,0:T(8,128)(2,1)}, u32[]{:S(2)}, u32[]{:S(2)}) collective-permute-start(bf16[2,1,1,128,768]{4,3,2,1,0:T(8,128)(2,1)S(1)} %pad_maximum_fusion), channel_id=1, source_target_pairs={{0,2},{1,3},{2,4},{3,5},{4,6},{5,7},{6,8},{7,9},{8,10},{9,11},{10,... | collective-permute-start | bytes 1179656 | tf_op jit(solution)/shard_map/ppermute | solution.py:19
  21.4 52.1 %collective-permute-start.2 = (bf16[2,1,1,128,768]{4,3,2,1,0:T(8,128)(2,1)S(1)}, bf16[2,1,1,128,768]{4,3,2,1,0:T(8,128)(2,1)}, u32[]{:S(2)}, u32[]{:S(2)}) collective-permute-start(bf16[2,1,1,128,768]{4,3,2,1,0:T(8,128)(2,1)S(1)} %pad_maximum_fusion), channel_id=1, source_target_pairs={{0,1},{1,2},{2,3},{3,4},{4,5},{5,6},{6,7},{7,8},{8,9},{9,10},{10,1... | collective-permute-start | bytes 1179656 | tf_op jit(solution)/shard_map/ppermute | solution.py:19
  25.2 50.8 %collective-permute-start.3 = (bf16[2,1,1,128,768]{4,3,2,1,0:T(8,128)(2,1)S(1)}, bf16[2,1,1,128,768]{4,3,2,1,0:T(8,128)(2,1)S(1)}, u32[]{:S(2)}, u32[]{:S(2)}) collective-permute-start(bf16[2,1,1,128,768]{4,3,2,1,0:T(8,128)(2,1)S(1)} %pad_maximum_fusion), channel_id=1, source_target_pairs={{0,63},{1,0},{2,1},{3,2},{4,3},{5,4},{6,5},{7,6},{8,7},{9,8},{10,9... | collective-permute-start | bytes 1179656 | tf_op jit(solution)/shard_map/ppermute | solution.py:19
  30.6 46.3 %collective-permute-start.4 = (bf16[2,1,1,128,768]{4,3,2,1,0:T(8,128)(2,1)S(1)}, bf16[2,1,1,128,768]{4,3,2,1,0:T(8,128)(2,1)S(1)}, u32[]{:S(2)}, u32[]{:S(2)}) collective-permute-start(bf16[2,1,1,128,768]{4,3,2,1,0:T(8,128)(2,1)S(1)} %pad_maximum_fusion), channel_id=1, source_target_pairs={{0,62},{1,63},{2,0},{3,1},{4,2},{5,3},{6,4},{7,5},{8,6},{9,7},{10,... | collective-permute-start | bytes 1179656 | tf_op jit(solution)/shard_map/ppermute | solution.py:19
  48.4 30.1 %collective-permute-start.5 = (bf16[2,1,1,128,768]{4,3,2,1,0:T(8,128)(2,1)S(1)}, bf16[2,1,1,128,768]{4,3,2,1,0:T(8,128)(2,1)S(1)}, u32[]{:S(2)}, u32[]{:S(2)}) collective-permute-start(bf16[2,1,1,128,768]{4,3,2,1,0:T(8,128)(2,1)S(1)} %pad_maximum_fusion), channel_id=1, source_target_pairs={{0,61},{1,62},{2,63},{3,0},{4,1},{5,2},{6,3},{7,4},{8,5},{9,6},{10... | collective-permute-start | bytes 1179656 | tf_op jit(solution)/shard_map/ppermute | solution.py:19
  102.4 6.7 %slice-start = ((s8[5505024]{0:T(1024)(128)(4,1)}), s8[4194304]{0:T(1024)(128)(4,1)S(1)}, s32[]{:S(2)}) async-start(s8[5505024]{0:T(1024)(128)(4,1)} %bitcast.81), calls=%async_computation.2 | async-start | bytes 8388608
  105.7 2.7 copy-start.3
  105.7 3.4 slice-start.1
  120.7 4.2 copy-start.4
  158.9 38.8 %copy-start.1 = (bf16[12,128,896]{1,2,0:T(8,128)(2,1)S(1)}, bf16[12,128,896]{1,2,0:T(8,128)(2,1)}, u32[]{:S(2)}) copy-start(bf16[12,128,896]{1,2,0:T(8,128)(2,1)} %multiply_convert_fusion) | copy-start | bytes 8257540
  158.9 38.8 %copy-start.2 = (bf16[896,12,64]{0,2,1:T(8,128)(2,1)S(1)}, bf16[896,12,64]{0,2,1:T(8,128)(2,1)}, u32[]{:S(2)}) copy-start(bf16[896,12,64]{0,2,1:T(8,128)(2,1)} %squeeze.37) | copy-start | bytes 4128772
  160.0 35.8 %collective-permute-start.11 = (bf16[2,1,1,128,768]{4,3,2,0,1:T(8,128)(2,1)S(1)}, bf16[2,1,1,128,768]{4,3,2,0,1:T(8,128)(2,1)S(1)}, u32[]{:S(2)}, u32[]{:S(2)}) collective-permute-start(bf16[2,1,1,128,768]{4,3,2,0,1:T(8,128)(2,1)S(1)} %get-tuple-element.48), channel_id=1, source_target_pairs={{0,3},{1,4},{2,5},{3,6},{4,7},{5,8},{6,9},{7,10},{8,11},{9,12},{10... | collective-permute-start | bytes 1179656 | tf_op jit(solution)/shard_map/ppermute | solution.py:19
  162.7 47.5 %collective-permute-start.10 = (bf16[2,1,1,128,768]{4,3,2,0,1:T(8,128)(2,1)}, bf16[2,1,1,128,768]{4,3,2,0,1:T(8,128)(2,1)S(1)}, u32[]{:S(2)}, u32[]{:S(2)}) collective-permute-start(bf16[2,1,1,128,768]{4,3,2,0,1:T(8,128)(2,1)} %get-tuple-element.49), channel_id=1, source_target_pairs={{0,2},{1,3},{2,4},{3,5},{4,6},{5,7},{6,8},{7,9},{8,10},{9,11},{10,... | collective-permute-start | bytes 1179656 | tf_op jit(solution)/shard_map/ppermute | solution.py:19
  173.2 46.8 %collective-permute-start.9 = (bf16[2,1,1,128,768]{4,3,2,0,1:T(8,128)(2,1)}, bf16[2,1,1,128,768]{4,3,2,0,1:T(8,128)(2,1)S(1)}, u32[]{:S(2)}, u32[]{:S(2)}) collective-permute-start(bf16[2,1,1,128,768]{4,3,2,0,1:T(8,128)(2,1)} %get-tuple-element.50), channel_id=1, source_target_pairs={{0,1},{1,2},{2,3},{3,4},{4,5},{5,6},{6,7},{7,8},{8,9},{9,10},{10,1... | collective-permute-start | bytes 1179656 | tf_op jit(solution)/shard_map/ppermute | solution.py:19
  175.5 44.5 %collective-permute-start.8 = (bf16[2,1,1,128,768]{4,3,2,0,1:T(8,128)(2,1)}, bf16[2,1,1,128,768]{4,3,2,0,1:T(8,128)(2,1)}, u32[]{:S(2)}, u32[]{:S(2)}) collective-permute-start(bf16[2,1,1,128,768]{4,3,2,0,1:T(8,128)(2,1)} %get-tuple-element.51), channel_id=1, source_target_pairs={{0,63},{1,0},{2,1},{3,2},{4,3},{5,4},{6,5},{7,6},{8,7},{9,8},{10,9... | collective-permute-start | bytes 1179656 | tf_op jit(solution)/shard_map/ppermute | solution.py:19
  182.4 37.6 %collective-permute-start.7 = (bf16[2,1,1,128,768]{4,3,2,0,1:T(8,128)(2,1)S(1)}, bf16[2,1,1,128,768]{4,3,2,0,1:T(8,128)(2,1)}, u32[]{:S(2)}, u32[]{:S(2)}) collective-permute-start(bf16[2,1,1,128,768]{4,3,2,0,1:T(8,128)(2,1)S(1)} %get-tuple-element.52), channel_id=1, source_target_pairs={{0,62},{1,63},{2,0},{3,1},{4,2},{5,3},{6,4},{7,5},{8,6},{9,7},{10,... | collective-permute-start | bytes 1179656 | tf_op jit(solution)/shard_map/ppermute | solution.py:19
  195.8 32.1 %collective-permute-start.6 = (bf16[2,1,1,128,768]{4,3,2,0,1:T(8,128)(2,1)S(1)}, bf16[2,1,1,128,768]{4,3,2,0,1:T(8,128)(2,1)}, u32[]{:S(2)}, u32[]{:S(2)}) collective-permute-start(bf16[2,1,1,128,768]{4,3,2,0,1:T(8,128)(2,1)S(1)} %get-tuple-element.47), channel_id=1, source_target_pairs={{0,61},{1,62},{2,63},{3,0},{4,1},{5,2},{6,3},{7,4},{8,5},{9,6},{10... | collective-permute-start | bytes 1179656 | tf_op jit(solution)/shard_map/ppermute | solution.py:19
Sparse Core Ops, SparseCore 0:
  126.5 36.0 reduce-scatter.1
where the time goes:
time: 523 us; the launch traced here: 522 us
  blocking collectives  284 us (54%)
  waiting for transfers between devices  67 us (13%)
  starting transfers between devices  56.1 us (11%)
  local copies, waits for them, and re-layouts  44.7 us (9%)
  other arithmetic  34.6 us (7%)
  matrix products  21.4 us (4%)
  between operations  14.3 us (3%)
    psum x1, blocking collectives, local(): grad_weight = lax.psum(grad_weight, 'station')  284 us
    ppermute x12, waiting for transfers between devices, from_behind(): return lax.ppermute(value, axis, pairs)  67 us
    ppermute x12, starting transfers between devices, from_behind(): return lax.ppermute(value, axis, pairs)  56 us
    another operation x3, local copies, waits for them, and re-layouts, one_station(): jnp.stack([key_part, value_part], 0).reshape(2, -1, span_rows, model_width)  14.7 us
    scatter-add x1, other arithmetic, local(): spread = jnp.zeros((2, window_count, candidates, span_rows, model_width),...  14.2 us
  transfers between devices with their start and end apart: 13, of which 8 were waited for; matrix products, arithmetic and copies ran while one was open for 10% of the time, Pallas kernels for 0%

commit v1 on v0

v1 whole, which is shorter than its diff:
```python
import math

import jax
import jax.numpy as jnp
from jax import lax
from jax.experimental import pallas as pl
from jax.experimental.pallas import tpu as pltpu
from jax.sharding import PartitionSpec as P

HEADS = 12
PMAX = 6
HOPS = 3
SPAN = 128
D = 768
PAIRS = HEADS // 2
STATIONS = 64
ZDIM = 16
XDIM = 4
YDIM = 4
GROUP = 4
DP = 8
ROWS = D // DP
MESH = pl.DeviceIdType.MESH
BF = jnp.bfloat16
F32 = jnp.float32
dead_bias = -1e30
KEY, VALUE, GRAD, QUERY = 0, 1, 2, 3


def dot(a, b, ca=1, cb=0):
    return lax.dot_general(a, b, (((ca,), (cb,)), ((), ())), preferred_element_type=F32)


def kernel(
    ids, cnt, q_ref, k_ref, v_ref, g_ref, w_ref,
    lo_ref, dq_ref, dk_ref, dv_ref, gw_ref,
    gat, kt, vt, s_buf, bdq, bdm, mixed_t, dq_t, stat, acc_k, acc_v,
    gwp, w1r, w2s, w2r, xs, xr, z1s, z1r, z2s, z2r, fin, xfin,
    send, recv,
):
    dp = lax.axis_index("dp")
    me = lax.axis_index("station")
    y, core = dp // 2, dp % 2
    x, z = me // ZDIM, me % ZDIM
    za, zb = z // GROUP, z % GROUP

    def station(offset):
        return (dp, lax.rem(me + offset + STATIONS, STATIONS))

    core_peer = (y * 2 + (1 - core), me)
    y_peers = [(lax.rem(y + o, YDIM) * 2 + core, me) for o in (1, 2, 3)]
    x_peers = [(dp, lax.rem(x + o, XDIM) * ZDIM + z) for o in (1, 2, 3)]
    zb_peers = [(dp, x * ZDIM + za * GROUP + lax.rem(zb + o, GROUP)) for o in (1, 2, 3)]
    za_peers = [(dp, x * ZDIM + lax.rem(za + o, GROUP) * GROUP + zb) for o in (1, 2, 3)]
    near = [station(o) for o in (1, 2, 3, -1, -2, -3)]
    greet = [core_peer] + y_peers + x_peers + zb_peers + za_peers + near
    barrier = pltpu.get_barrier_semaphore()
    for peer in greet:
        pl.semaphore_signal(barrier, inc=1, device_id=peer, device_id_type=MESH)
    pl.semaphore_wait(barrier, len(greet))

    started = []

    def remote(src, dst, number, peer):
        copy = pltpu.make_async_remote_copy(
            src_ref=src, dst_ref=dst, send_sem=send.at[number], recv_sem=recv.at[number],
            device_id=peer, device_id_type=MESH,
        )
        copy.start()
        started.append(copy)
        return copy

    own = (k_ref, v_ref, g_ref, q_ref)
    flights = {}

    def hop(item, h):
        for way in (0, 1):
            src = own[item] if h == 1 else gat.at[item, way, h - 2]
            flights[item, way, h] = remote(
                src, gat.at[item, way, h - 1], (item * 2 + way) * 3 + h - 1,
                station(1 if way == 0 else -1),
            )

    def arrived(item, h):
        for way in (0, 1):
            flights[item, way, h].wait_recv()

    def block(item, j):
        if j == 0:
            return own[item]
        return gat.at[item, (j - 1) // 3, (j - 1) % 3]

    hop(KEY, 1)
    hop(VALUE, 1)

    offsets = (0, -1, -2, -3, 1, 2, 3)

    def listed(reader, block_station):
        hit = jnp.int32(0)
        for p in range(PMAX):
            same = ids[reader, p] == block_station
            live = p < cnt[reader]
            hit = hit + jnp.where(same & live, jnp.int32(1), jnp.int32(0))
        return jnp.where(hit > 0, F32(0.0), F32(dead_bias))

    bias_f, bias_b = [F32(0.0)], [F32(0.0)]
    for o in offsets[1:]:
        other = station(o)[1]
        bias_f.append(listed(me, other))
        bias_b.append(listed(other, me))

    bdq[...] = jnp.zeros_like(bdq)
    bdm[...] = jnp.zeros_like(bdm)

    def prepare(j, slot):
        q_t = block(QUERY, j)[...].T
        q_t = (q_t.astype(F32) * 0.125).astype(BF)
        m_t = dot(w_ref[...], block(GRAD, j)[...], 1, 1).astype(BF)
        for p in range(PAIRS):
            a, b = p * 128, p * 128 + 64
            bdq[slot, p, 0:64, 0:128] = q_t[a : a + 64]
            bdq[slot, p, 64:128, 128:256] = q_t[b : b + 64]
            bdm[slot, p, 0:64, 0:128] = m_t[a : a + 64]
            bdm[slot, p, 64:128, 128:256] = m_t[b : b + 64]

    def turn(j):
        kt[j] = block(KEY, j)[...].T
        vt[j] = block(VALUE, j)[...].T

    prepare(0, 0)
    turn(0)
    for h in (1, 2):
        for item in (KEY, VALUE):
            arrived(item, h)
            hop(item, h + 1)
        if h == 2:
            hop(GRAD, 1)
            hop(QUERY, 1)
        turn(h)
        turn(3 + h)
    arrived(KEY, 3)
    arrived(VALUE, 3)
    turn(3)
    turn(6)

    def forward(p, carry):
        cols = pl.ds(pl.multiple_of(p * 128, 128), 128)
        rhs_q, rhs_m = bdq[0, p], bdm[0, p]
        top = None
        for j in range(7):
            s = dot(block(KEY, j)[:, cols], rhs_q) + bias_f[j]
            s_buf[j] = s
            m = jnp.max(s, 0, keepdims=True)
            top = m if top is None else jnp.maximum(top, m)
        total = jnp.zeros_like(top)
        for j in range(7):
            e = jnp.exp(s_buf[j] - top)
            s_buf[j] = e
            total = total + jnp.sum(e, 0, keepdims=True)
        inv = 1.0 / total
        out = jnp.zeros((128, 256), F32)
        for j in range(7):
            prob = s_buf[j] * inv
            s_buf[j] = prob
            out = out + dot(vt[j, cols, :], prob.astype(BF))
        out = out.astype(BF)
        mixed_t[pl.ds(pl.multiple_of(p * 128, 128), 64), :] = out[0:64, 0:128]
        mixed_t[pl.ds(pl.multiple_of(p * 128 + 64, 64), 64), :] = out[64:128, 128:256]
        delta = jnp.sum(rhs_m.astype(F32) * out.astype(F32), 0, keepdims=True)
        stat[0, pl.ds(p, 1), :] = top + jnp.log(total)
        stat[0, pl.ds(p + 8, 1), :] = delta
        grad = jnp.zeros((128, 256), F32)
        for j in range(7):
            d_prob = dot(block(VALUE, j)[:, cols], rhs_m)
            d_score = (s_buf[j] * (d_prob - delta)).astype(BF)
            grad = grad + dot(kt[j, cols, :], d_score)
        grad = (grad * 0.125).astype(BF)
        dq_t[pl.ds(pl.multiple_of(p * 128, 128), 64), :] = grad[0:64, 0:128]
        dq_t[pl.ds(pl.multiple_of(p * 128 + 64, 64), 64), :] = grad[64:128, 128:256]
        return carry

    lax.fori_loop(0, 4, forward, 0)
    arrived(GRAD, 1)
    hop(GRAD, 2)
    lax.fori_loop(4, PAIRS, forward, 0)

    for d in range(DP):
        rows = mixed_t[d * ROWS : (d + 1) * ROWS, :]
        gwp[d % 2, d // 2] = dot(rows, g_ref[...]).astype(BF)
    stats = []
    for d in (1, 2, 3):
        stats.append(remote(stat.at[0], stat.at[d], 24 + d - 1, station(d)))
        stats.append(remote(stat.at[0], stat.at[3 + d], 27 + d - 1, station(-d)))
    core_copy = remote(gwp.at[1 - core], w1r, 30, core_peer)
    arrived(QUERY, 1)
    hop(QUERY, 2)
    lo_ref[...] = dot(mixed_t[...].T, w_ref[...]).astype(BF)
    dq_ref[...] = dq_t[...].T

    core_copy.wait_recv()
    for n in range(YDIM):
        w2s[n] = (gwp[core, n].astype(F32) + w1r[n].astype(F32)).astype(BF)
    y_copies = [
        remote(w2s.at[lax.rem(y + o, YDIM)], w2r.at[o - 1], 31 + o - 1, y_peers[o - 1])
        for o in (1, 2, 3)
    ]

    acc_k[...] = jnp.zeros_like(acc_k)
    acc_v[...] = jnp.zeros_like(acc_v)

    def backward(j, slot):
        def step(p, carry):
            cols = pl.ds(pl.multiple_of(p * 128, 128), 128)
            rhs_q, rhs_m = bdq[slot, p], bdm[slot, p]
            shift = bias_b[j] - stat[j, pl.ds(p, 1), :]
            prob = jnp.exp(dot(k_ref[:, cols], rhs_q) + shift)
            d_prob = dot(v_ref[:, cols], rhs_m)
            d_score = (prob * (d_prob - stat[j, pl.ds(p + 8, 1), :])).astype(BF)
            acc_v[:, cols] += dot(prob.astype(BF), rhs_m, 1, 1)
            acc_k[:, cols] += dot(d_score, rhs_q, 1, 1)
            return carry

        lax.fori_loop(0, PAIRS, step, 0)

    backward(0, 0)
    arrived(GRAD, 2)
    hop(GRAD, 3)
    for copy in stats:
        copy.wait_recv()
    prepare(1, 1)
    backward(1, 1)
    arrived(QUERY, 2)
    hop(QUERY, 3)
    prepare(4, 0)
    backward(4, 0)

    for copy in y_copies:
        copy.wait_recv()
    total = w2s[y].astype(F32)
    for n in range(3):
        total = total + w2r[n].astype(F32)
    for n in range(XDIM):
        for r in range(3):
            lower = n * 24 + r * 8
            piece = total[lower : lower + 8]
            xs[n, r] = jnp.concatenate([piece[:, 0:384], piece[:, 384:768]], 0).astype(BF)
    x_copies = [
        remote(xs.at[lax.rem(x + o, XDIM)], xr.at[o - 1], 34 + o - 1, x_peers[o - 1])
        for o in (1, 2, 3)
    ]
    prepare(2, 1)
    backward(2, 1)

    for copy in x_copies:
        copy.wait_recv()
    part = xs[x].astype(F32)
    for n in range(3):
        part = part + xr[n].astype(F32)
    z1s[0:3] = part.astype(BF)
    z1s[3] = jnp.zeros_like(z1s[3])
    zb_copies = [
        remote(z1s.at[lax.rem(zb + o, GROUP)], z1r.at[o - 1], 37 + o - 1, zb_peers[o - 1])
        for o in (1, 2, 3)
    ]
    prepare(5, 0)
    backward(5, 0)

    for copy in zb_copies:
        copy.wait_recv()
    part = z1s[zb].astype(F32)
    for n in range(3):
        part = part + z1r[n].astype(F32)
    z2s[...] = part.astype(BF)
    za_copies = [remote(z2s, z2r.at[o - 1], 40 + o - 1, za_peers[o - 1]) for o in (1, 2, 3)]

    arrived(GRAD, 3)
    arrived(QUERY, 3)
    prepare(3, 1)
    backward(3, 1)
    prepare(6, 0)
    backward(6, 0)
    dk_ref[...] = acc_k[...].astype(BF)
    dv_ref[...] = acc_v[...].astype(BF)

    for copy in za_copies:
        copy.wait_recv()
    part = z2s[...].astype(F32)
    for n in range(3):
        part = part + z2r[n].astype(F32)
    fin[zb] = (part * (1.0 / math.sqrt(DP * STATIONS * SPAN))).astype(BF)
    zb_copies = [remote(fin.at[zb], fin.at[zb], 43 + o - 1, zb_peers[o - 1]) for o in (1, 2, 3)]
    for copy in zb_copies:
        copy.wait_recv()
    x_copies = [
        remote(fin.at[pl.ds(0, 3)], xfin.at[x], 46 + o - 1, x_peers[o - 1]) for o in (1, 2, 3)
    ]
    xfin[x] = fin[0:3]
    for copy in x_copies:
        copy.wait_recv()
    for n in range(XDIM):
        for r in range(3):
            lower = n * 24 + r * 8
            piece = xfin[n, r].astype(F32)
            gw_ref[lower : lower + 8, 0:384] = piece[0:8]
            gw_ref[lower : lower + 8, 384:768] = piece[8:16]
    for copy in started:
        copy.wait_send()


def local(
    query_states, key_states, value_states, grad_output, out_weight, partner_ids, partner_count
):
    shape = query_states.shape
    flat = [a.reshape(SPAN, D) for a in (query_states, key_states, value_states, grad_output)]
    vmem = pl.BlockSpec(memory_space=pltpu.VMEM)
    smem = pl.BlockSpec(memory_space=pltpu.SMEM)
    rows = jax.ShapeDtypeStruct((SPAN, D), BF)
    copies = 49
    outs = pl.pallas_call(
        kernel,
        out_shape=(rows, rows, rows, rows, jax.ShapeDtypeStruct((ROWS, D), F32)),
        in_specs=[smem, smem] + [vmem] * 5,
        out_specs=(vmem,) * 5,
        scratch_shapes=[
            pltpu.VMEM((4, 2, HOPS, SPAN, D), BF),
            pltpu.VMEM((7, D, SPAN), BF),
            pltpu.VMEM((7, D, SPAN), BF),
            pltpu.VMEM((7, SPAN, 256), F32),
            pltpu.VMEM((2, PAIRS, 128, 256), BF),
            pltpu.VMEM((2, PAIRS, 128, 256), BF),
            pltpu.VMEM((D, SPAN), BF),
            pltpu.VMEM((D, SPAN), BF),
            pltpu.VMEM((7, 16, 256), F32),
            pltpu.VMEM((SPAN, D), F32),
            pltpu.VMEM((SPAN, D), F32),
            pltpu.VMEM((2, YDIM, ROWS, D), BF),
            pltpu.VMEM((YDIM, ROWS, D), BF),
            pltpu.VMEM((YDIM, ROWS, D), BF),
            pltpu.VMEM((3, ROWS, D), BF),
            pltpu.VMEM((XDIM, 3, 16, 384), BF),
            pltpu.VMEM((3, 3, 16, 384), BF),
            pltpu.VMEM((GROUP, 16, 384), BF),
            pltpu.VMEM((3, 16, 384), BF),
            pltpu.VMEM((16, 384), BF),
            pltpu.VMEM((3, 16, 384), BF),
            pltpu.VMEM((GROUP, 16, 384), BF),
            pltpu.VMEM((XDIM, 3, 16, 384), BF),
            pltpu.SemaphoreType.DMA((copies,)),
            pltpu.SemaphoreType.DMA((copies,)),
        ],
        compiler_params=pltpu.CompilerParams(
            collective_id=0, has_side_effects=True, vmem_limit_bytes=48 * 1024 * 1024
        ),
    )(partner_ids, partner_count, *flat, out_weight)
    return tuple(a.reshape(shape) for a in outs[:4]) + (outs[4],)


def solution(mesh):
    tokens = P("dp", "station", None, None)
    return jax.shard_map(
        local,
        mesh=mesh,
        in_specs=(tokens,) * 4 + (P(), P(), P()),
        out_specs=(tokens,) * 4 + (P("dp", None),),
        check_vma=False,
    )
```

time: 523 us -> 102 us (0.20)
  blocking collectives: 284 us -> 0 us
  Pallas kernels: 0 us -> 91.4 us
  waiting for transfers between devices: 67 us -> 0 us
  starting transfers between devices: 56.1 us -> 0 us
  local copies, waits for them, and re-layouts: 44.7 us -> 9.83 us
  other arithmetic: 34.6 us -> 0 us
  matrix products: 21.4 us -> 0 us
  between operations: 14.3 us -> 0.65 us
    psum x1 -> x0, blocking collectives: 284 us -> none  [local(): grad_weight = lax.psum(grad_weight, 'station')]
    pallas_call x0 -> x1, Pallas kernels: none -> 91.4 us  [local(): pl.pallas_call(kernel, out_shape=(rows, rows, rows, rows, jax.ShapeDtypeS...]
    ppermute x12 -> x0, waiting for transfers between devices: 67 us -> none  [from_behind(): return lax.ppermute(value, axis, pairs)]
    ppermute x12 -> x0, starting transfers between devices: 56 us -> none  [from_behind(): return lax.ppermute(value, axis, pairs)]
    dot_general x8 -> x0, matrix products: 15.4 us -> none  [the longest x1 4.5 us: one_station(): jnp.einsum('hqk,qhd->khd', grad_scores, query_rows, preferred_element_typ...]
    another operation x3 -> x0, local copies, waits for them, and re-layouts: 14.7 us -> none  [one_station(): jnp.stack([key_part, value_part], 0).reshape(2, -1, span_rows, model_width)]
    scatter-add x1 -> x0, other arithmetic: 14.2 us -> none  [local(): spread = jnp.zeros((2, window_count, candidates, span_rows, model_width),...]
    another operation x4 -> x0, other arithmetic: 12 us -> none  [the longest x1 6.11 us: one_station(): jnp.stack([key_part, value_part], 0).reshape(2, -1, span_rows, model_width)]
  transfers between devices with their start and end apart: 13 -> 0, of which waited for: 8 -> 0; matrix products, arithmetic and copies ran while one was open for 10% -> 0% of each run, Pallas kernels for 0% -> 0%
where the time goes in v1:
time: 102 us
  Pallas kernels  91.4 us (90%)
  local copies, waits for them, and re-layouts  9.83 us (10%)
    pallas_call x1, Pallas kernels, local(): pl.pallas_call(kernel, out_shape=(rows, rows, rows, rows, jax.ShapeDtypeS...  91.4 us
    unnamed x18, local copies, waits for them, and re-layouts  9.83 us

profile of v1, /device:TPU:24, one launch (start us, length us, event | category | flops | bytes accessed | tf_op | source)
XLA Modules:
  0.0 101.9 jit_solution(5800750327168415119)
XLA Ops:
  0.6 0.8 copy.12.ids
  1.4 0.0 copy-start
  1.4 1.3 %copy-done = bf16[768,768]{1,0:T(8,128)(2,1)S(1)} copy-done((bf16[768,768]{1,0:T(8,128)(2,1)S(1)}, bf16[768,768]{1,0:T(8,128)(2,1)}, u32[]{:S(2)}) %copy-start) | copy-done | bytes 1179672
  2.7 0.0 copy-start.1
  2.7 0.9 copy-done.1
  3.6 0.0 copy-start.2
  3.6 0.9 copy-done.2
  4.5 0.0 copy-start.3
  4.5 0.9 copy-done.3
  5.5 0.0 copy-start.4
  5.5 0.9 copy-done.4
  6.4 0.0 copy-start.5
  6.4 0.7 copy-done.5
  7.0 91.4 %shard_map.110 = (bf16[128,768]{1,0:T(8,128)(2,1)S(1)}, bf16[128,768]{1,0:T(8,128)(2,1)S(1)}, bf16[128,768]{1,0:T(8,128)(2,1)S(1)}, bf16[128,768]{1,0:T(8,128)(2,1)S(1)}, f32[96,768]{1,0:T(8,128)S(1)}) custom-call(s32[64,6]{1,0:T(8,128)S(1)} %copy.12.ids, s32[64]{0:T(128)S(1)} %copy-done.5, bf16[128,768]{1,0:T(8,128)(2,1)S(1)} %bitcast.8, ...), custom_call_target="tpu_custom_call" | custom-call | tf_op jit(solution)/shard_map/pallas_call | solution.py:319
  98.4 0.7 copy.18
  99.1 0.7 copy.19
  99.8 0.7 copy.20
  100.5 0.7 copy.21
  101.1 0.7 copy.22
Async XLA Ops:
  1.4 1.3 %copy-start = (bf16[768,768]{1,0:T(8,128)(2,1)S(1)}, bf16[768,768]{1,0:T(8,128)(2,1)}, u32[]{:S(2)}) copy-start(bf16[768,768]{1,0:T(8,128)(2,1)} %w_ref.1) | copy-start | bytes 3538948
  2.7 0.9 copy-start.1
  3.6 0.9 copy-start.2
  4.5 0.9 copy-start.3
  5.5 0.9 copy-start.4
  6.4 0.7 copy-start.5

commit v2 on v1

--- a/solution.py
+++ b/solution.py
@@ -32,12 +32,21 @@
 
 
 def kernel(
-    ids, cnt, q_ref, k_ref, v_ref, g_ref, w_ref,
-    lo_ref, dq_ref, dk_ref, dv_ref, gw_ref,
+    ids, cnt, q_in, k_in, v_in, g_in, w_in,
+    lo_out, dq_out, dk_out, dv_out, gw_out,
     gat, kt, vt, s_buf, bdq, bdm, mixed_t, dq_t, stat, acc_k, acc_v,
     gwp, w1r, w2s, w2r, xs, xr, z1s, z1r, z2s, z2r, fin, xfin,
-    send, recv,
+    q_ref, k_ref, v_ref, g_ref, w_ref,
+    lo_ref, dq_ref, dk_ref, dv_ref, gw_ref, load, put, send, recv,
 ):
+    loads = [
+        pltpu.make_async_copy(src, dst, load.at[n])
+        for n, (src, dst) in enumerate(
+            ((w_in, w_ref), (g_in, g_ref), (q_in, q_ref), (k_in, k_ref), (v_in, v_ref))
+        )
+    ]
+    for copy in loads:
+        copy.start()
     dp = lax.axis_index("dp")
     me = lax.axis_index("station")
     y, core = dp // 2, dp % 2
@@ -70,12 +79,19 @@
         started.append(copy)
         return copy
 
+    source = (k_in, v_in, g_in, q_in)
     own = (k_ref, v_ref, g_ref, q_ref)
     flights = {}
+    puts = []
+
+    def store(n, src, dst):
+        copy = pltpu.make_async_copy(src, dst, put.at[n])
+        copy.start()
+        puts.append(copy)
 
     def hop(item, h):
         for way in (0, 1):
-            src = own[item] if h == 1 else gat.at[item, way, h - 2]
+            src = source[item] if h == 1 else gat.at[item, way, h - 2]
             flights[item, way, h] = remote(
                 src, gat.at[item, way, h - 1], (item * 2 + way) * 3 + h - 1,
                 station(1 if way == 0 else -1),
@@ -111,6 +127,8 @@
 
     bdq[...] = jnp.zeros_like(bdq)
     bdm[...] = jnp.zeros_like(bdm)
+    for copy in loads:
+        copy.wait()
 
     def prepare(j, slot):
         q_t = block(QUERY, j)[...].T
@@ -187,15 +205,15 @@
     for d in range(DP):
         rows = mixed_t[d * ROWS : (d + 1) * ROWS, :]
         gwp[d % 2, d // 2] = dot(rows, g_ref[...]).astype(BF)
+    core_copy = remote(gwp.at[1 - core], w1r, 30, core_peer)
     stats = []
     for d in (1, 2, 3):
         stats.append(remote(stat.at[0], stat.at[d], 24 + d - 1, station(d)))
         stats.append(remote(stat.at[0], stat.at[3 + d], 27 + d - 1, station(-d)))
-    core_copy = remote(gwp.at[1 - core], w1r, 30, core_peer)
     arrived(QUERY, 1)
     hop(QUERY, 2)
     lo_ref[...] = dot(mixed_t[...].T, w_ref[...]).astype(BF)
-    dq_ref[...] = dq_t[...].T
+    store(0, lo_ref, lo_out)
 
     core_copy.wait_recv()
     for n in range(YDIM):
@@ -205,6 +223,8 @@
         for o in (1, 2, 3)
     ]
 
+    dq_ref[...] = dq_t[...].T
+    store(1, dq_ref, dq_out)
     acc_k[...] = jnp.zeros_like(acc_k)
     acc_v[...] = jnp.zeros_like(acc_v)
 
@@ -281,6 +301,8 @@
     backward(6, 0)
     dk_ref[...] = acc_k[...].astype(BF)
     dv_ref[...] = acc_v[...].astype(BF)
+    store(2, dk_ref, dk_out)
+    store(3, dv_ref, dv_out)
 
     for copy in za_copies:
         copy.wait_recv()
@@ -303,8 +325,11 @@
             piece = xfin[n, r].astype(F32)
             gw_ref[lower : lower + 8, 0:384] = piece[0:8]
             gw_ref[lower : lower + 8, 384:768] = piece[8:16]
+    store(4, gw_ref, gw_out)
     for copy in started:
         copy.wait_send()
+    for copy in puts:
+        copy.wait()
 
 
 def local(
@@ -312,15 +337,15 @@
 ):
     shape = query_states.shape
     flat = [a.reshape(SPAN, D) for a in (query_states, key_states, value_states, grad_output)]
-    vmem = pl.BlockSpec(memory_space=pltpu.VMEM)
+    hbm = pl.BlockSpec(memory_space=pl.ANY)
     smem = pl.BlockSpec(memory_space=pltpu.SMEM)
     rows = jax.ShapeDtypeStruct((SPAN, D), BF)
     copies = 49
     outs = pl.pallas_call(
         kernel,
         out_shape=(rows, rows, rows, rows, jax.ShapeDtypeStruct((ROWS, D), F32)),
-        in_specs=[smem, smem] + [vmem] * 5,
-        out_specs=(vmem,) * 5,
+        in_specs=[smem, smem] + [hbm] * 5,
+        out_specs=(hbm,) * 5,
         scratch_shapes=[
             pltpu.VMEM((4, 2, HOPS, SPAN, D), BF),
             pltpu.VMEM((7, D, SPAN), BF),
@@ -345,11 +370,23 @@
             pltpu.VMEM((3, 16, 384), BF),
             pltpu.VMEM((GROUP, 16, 384), BF),
             pltpu.VMEM((XDIM, 3, 16, 384), BF),
+            pltpu.VMEM((SPAN, D), BF),
+            pltpu.VMEM((SPAN, D), BF),
+            pltpu.VMEM((SPAN, D), BF),
+            pltpu.VMEM((SPAN, D), BF),
+            pltpu.VMEM((D, D), BF),
+            pltpu.VMEM((SPAN, D), BF),
+            pltpu.VMEM((SPAN, D), BF),
+            pltpu.VMEM((SPAN, D), BF),
+            pltpu.VMEM((SPAN, D), BF),
+            pltpu.VMEM((ROWS, D), F32),
+            pltpu.SemaphoreType.DMA((5,)),
+            pltpu.SemaphoreType.DMA((5,)),
             pltpu.SemaphoreType.DMA((copies,)),
             pltpu.SemaphoreType.DMA((copies,)),
         ],
         compiler_params=pltpu.CompilerParams(
-            collective_id=0, has_side_effects=True, vmem_limit_bytes=48 * 1024 * 1024
+            collective_id=0, has_side_effects=True, vmem_limit_bytes=67043328
         ),
     )(partner_ids, partner_count, *flat, out_weight)
     return tuple(a.reshape(shape) for a in outs[:4]) + (outs[4],)

time: 102 us -> 101 us (level)
  local copies, waits for them, and re-layouts: 9.83 us -> 7.69 us
  Pallas kernels: 91.4 us -> 92.5 us
    unnamed x18 -> x10, local copies, waits for them, and re-layouts: 9.83 us -> 7.69 us
    pallas_call x1, Pallas kernels: 91.4 us -> 92.5 us  [local(): pl.pallas_call(kernel, out_shape=(rows, rows, rows, rows, jax.ShapeDtypeS...]
where the time goes in v2:
time: 101 us
  Pallas kernels  92.5 us (92%)
  local copies, waits for them, and re-layouts  7.69 us (8%)
    pallas_call x1, Pallas kernels, local(): pl.pallas_call(kernel, out_shape=(rows, rows, rows, rows, jax.ShapeDtypeS...  92.5 us
    unnamed x10, local copies, waits for them, and re-layouts  7.69 us

profile of v2, /device:TPU:24, one launch (start us, length us, event | category | flops | bytes accessed | tf_op | source)
XLA Modules:
  0.0 100.8 jit_solution(10428952791297195173)
XLA Ops:
  0.6 1.4 %copy.12.ids = s32[64,6]{1,0:T(8,128)} copy(s32[64,6]{0,1:T(8,128)} %param.12) | data formatting | bytes 3072 | tf_op args[5]
  2.0 92.5 %shard_map.110 = (bf16[128,768]{1,0:T(8,128)(2,1)}, bf16[128,768]{1,0:T(8,128)(2,1)}, bf16[128,768]{1,0:T(8,128)(2,1)}, bf16[128,768]{1,0:T(8,128)(2,1)}, f32[96,768]{1,0:T(8,128)}) custom-call(s32[64,6]{1,0:T(8,128)} %copy.12.ids, s32[64]{0:T(128)} %cnt.1, bf16[128,768]{1,0:T(8,128)(2,1)} %bitcast.8, bf16[128,768]{1,0:T(8,128)(2,1)} %bitcast.9, ...), custom_call_target="tpu_custom_call" | custom-call | tf_op jit(solution)/shard_map/pallas_call | solution.py:344
  94.5 0.0 copy-start.1
  94.5 0.0 copy-start
  94.5 1.7 %copy.18 = bf16[1,1,128,768]{3,2,1,0:T(8,128)(2,1)} copy(bf16[1,1,128,768]{3,2,1,0:T(8,128)(2,1)} %bitcast.15) | data formatting | bytes 393216
  96.2 1.6 %copy.19 = bf16[1,1,128,768]{3,2,1,0:T(8,128)(2,1)} copy(bf16[1,1,128,768]{3,2,1,0:T(8,128)(2,1)} %bitcast.14) | data formatting | bytes 393216
  97.8 1.6 %copy.20 = bf16[1,1,128,768]{3,2,1,0:T(8,128)(2,1)} copy(bf16[1,1,128,768]{3,2,1,0:T(8,128)(2,1)} %bitcast.13) | data formatting | bytes 393216
  99.4 0.0 copy-done.1
  99.4 0.7 copy.21
  100.1 0.0 copy-done
  100.1 0.7 copy.22
Async XLA Ops:
  94.5 4.9 %copy-start.1 = (bf16[128,768]{1,0:T(8,128)(2,1)S(1)}, bf16[128,768]{1,0:T(8,128)(2,1)}, u32[]{:S(2)}) copy-start(bf16[128,768]{1,0:T(8,128)(2,1)} %get-tuple-element.13) | copy-start | bytes 589828
  94.5 5.6 %copy-start = (f32[96,768]{1,0:T(8,128)S(1)}, f32[96,768]{1,0:T(8,128)}, u32[]{:S(2)}) copy-start(f32[96,768]{1,0:T(8,128)} %get-tuple-element.24) | copy-start | bytes 884740

commit v3 on v2

--- a/solution.py
+++ b/solution.py
@@ -33,11 +33,11 @@
 
 def kernel(
     ids, cnt, q_in, k_in, v_in, g_in, w_in,
-    lo_out, dq_out, dk_out, dv_out, gw_out,
+    lo_ref, dq_ref, dk_ref, dv_ref, gw_ref,
     gat, kt, vt, s_buf, bdq, bdm, mixed_t, dq_t, stat, acc_k, acc_v,
-    gwp, w1r, w2s, w2r, xs, xr, z1s, z1r, z2s, z2r, fin, xfin,
+    gwp, w1r, ys_a, yr_a, xs_b, xr_b, xs_a, xr_a, ys_b, yr_b, z1s, z1r, z2s, z2r, fin, xfin,
     q_ref, k_ref, v_ref, g_ref, w_ref,
-    lo_ref, dq_ref, dk_ref, dv_ref, gw_ref, load, put, send, recv,
+    load, send, recv,
 ):
     loads = [
         pltpu.make_async_copy(src, dst, load.at[n])
@@ -82,12 +82,24 @@
     source = (k_in, v_in, g_in, q_in)
     own = (k_ref, v_ref, g_ref, q_ref)
     flights = {}
-    puts = []
-
-    def store(n, src, dst):
-        copy = pltpu.make_async_copy(src, dst, put.at[n])
-        copy.start()
-        puts.append(copy)
+
+    def spread(parts, landing, own_index, peers, number):
+        count = len(peers) + 1
+        return [
+            remote(
+                parts.at[lax.rem(own_index + o, count)], landing.at[o - 1],
+                number + o - 1, peers[o - 1],
+            )
+            for o in (1, 2, 3)
+        ]
+
+    def gathered(copies, parts, landing, own_index):
+        for copy in copies:
+            copy.wait_recv()
+        total = parts[own_index].astype(F32)
+        for n in range(3):
+            total = total + landing[n].astype(F32)
+        return total
 
     def hop(item, h):
         for way in (0, 1):
@@ -213,18 +225,19 @@
     arrived(QUERY, 1)
     hop(QUERY, 2)
     lo_ref[...] = dot(mixed_t[...].T, w_ref[...]).astype(BF)
-    store(0, lo_ref, lo_out)
 
     core_copy.wait_recv()
+    sums = [gwp[core, n].astype(F32) + w1r[n].astype(F32) for n in range(YDIM)]
     for n in range(YDIM):
-        w2s[n] = (gwp[core, n].astype(F32) + w1r[n].astype(F32)).astype(BF)
-    y_copies = [
-        remote(w2s.at[lax.rem(y + o, YDIM)], w2r.at[o - 1], 31 + o - 1, y_peers[o - 1])
-        for o in (1, 2, 3)
-    ]
+        ys_a[n] = sums[n][:, 0:384].astype(BF)
+    for n in range(XDIM):
+        xs_b[n] = jnp.concatenate(
+            [sums[m][n * 24 : n * 24 + 24, 384:768] for m in range(YDIM)], 0
+        ).astype(BF)
+    first_a = spread(ys_a, yr_a, y, y_peers, 31)
+    first_b = spread(xs_b, xr_b, x, x_peers, 34)
 
     dq_ref[...] = dq_t[...].T
-    store(1, dq_ref, dq_out)
     acc_k[...] = jnp.zeros_like(acc_k)
     acc_v[...] = jnp.zeros_like(acc_v)
 
@@ -251,39 +264,30 @@
     backward(1, 1)
     arrived(QUERY, 2)
     hop(QUERY, 3)
+    total = gathered(first_a, ys_a, yr_a, y)
+    for n in range(XDIM):
+        xs_a[n] = total[n * 24 : n * 24 + 24].astype(BF)
+    second_a = spread(xs_a, xr_a, x, x_peers, 49)
+    total = gathered(first_b, xs_b, xr_b, x)
+    for n in range(YDIM):
+        ys_b[n] = total[n * 24 : n * 24 + 24].astype(BF)
+    second_b = spread(ys_b, yr_b, y, y_peers, 52)
     prepare(4, 0)
     backward(4, 0)
 
-    for copy in y_copies:
-        copy.wait_recv()
-    total = w2s[y].astype(F32)
-    for n in range(3):
-        total = total + w2r[n].astype(F32)
-    for n in range(XDIM):
-        for r in range(3):
-            lower = n * 24 + r * 8
-            piece = total[lower : lower + 8]
-            xs[n, r] = jnp.concatenate([piece[:, 0:384], piece[:, 384:768]], 0).astype(BF)
-    x_copies = [
-        remote(xs.at[lax.rem(x + o, XDIM)], xr.at[o - 1], 34 + o - 1, x_peers[o - 1])
-        for o in (1, 2, 3)
-    ]
-    prepare(2, 1)
-    backward(2, 1)
-
-    for copy in x_copies:
-        copy.wait_recv()
-    part = xs[x].astype(F32)
-    for n in range(3):
-        part = part + xr[n].astype(F32)
-    z1s[0:3] = part.astype(BF)
+    half_a = gathered(second_a, xs_a, xr_a, x)
+    half_b = gathered(second_b, ys_b, yr_b, y)
+    for r in range(3):
+        z1s[r] = jnp.concatenate(
+            [half_a[r * 8 : r * 8 + 8], half_b[r * 8 : r * 8 + 8]], 0
+        ).astype(BF)
     z1s[3] = jnp.zeros_like(z1s[3])
     zb_copies = [
         remote(z1s.at[lax.rem(zb + o, GROUP)], z1r.at[o - 1], 37 + o - 1, zb_peers[o - 1])
         for o in (1, 2, 3)
     ]
-    prepare(5, 0)
-    backward(5, 0)
+    prepare(2, 1)
+    backward(2, 1)
 
     for copy in zb_copies:
         copy.wait_recv()
@@ -293,6 +297,8 @@
     z2s[...] = part.astype(BF)
     za_copies = [remote(z2s, z2r.at[o - 1], 40 + o - 1, za_peers[o - 1]) for o in (1, 2, 3)]
 
+    prepare(5, 0)
+    backward(5, 0)
     arrived(GRAD, 3)
     arrived(QUERY, 3)
     prepare(3, 1)
@@ -301,8 +307,6 @@
     backward(6, 0)
     dk_ref[...] = acc_k[...].astype(BF)
     dv_ref[...] = acc_v[...].astype(BF)
-    store(2, dk_ref, dk_out)
-    store(3, dv_ref, dv_out)
 
     for copy in za_copies:
         copy.wait_recv()
@@ -325,27 +329,29 @@
             piece = xfin[n, r].astype(F32)
             gw_ref[lower : lower + 8, 0:384] = piece[0:8]
             gw_ref[lower : lower + 8, 384:768] = piece[8:16]
-    store(4, gw_ref, gw_out)
     for copy in started:
         copy.wait_send()
-    for copy in puts:
-        copy.wait()
 
 
 def local(
     query_states, key_states, value_states, grad_output, out_weight, partner_ids, partner_count
 ):
     shape = query_states.shape
-    flat = [a.reshape(SPAN, D) for a in (query_states, key_states, value_states, grad_output)]
-    hbm = pl.BlockSpec(memory_space=pl.ANY)
+    flat = [
+        pltpu.with_memory_space_constraint(a.reshape(SPAN, D), pltpu.HBM)
+        for a in (query_states, key_states, value_states, grad_output)
+    ]
+    out_weight = pltpu.with_memory_space_constraint(out_weight, pltpu.HBM)
+    hbm = pl.BlockSpec(memory_space=pltpu.HBM)
+    vmem = pl.BlockSpec(memory_space=pltpu.VMEM)
     smem = pl.BlockSpec(memory_space=pltpu.SMEM)
     rows = jax.ShapeDtypeStruct((SPAN, D), BF)
-    copies = 49
+    copies = 55
     outs = pl.pallas_call(
         kernel,
         out_shape=(rows, rows, rows, rows, jax.ShapeDtypeStruct((ROWS, D), F32)),
         in_specs=[smem, smem] + [hbm] * 5,
-        out_specs=(hbm,) * 5,
+        out_specs=(vmem,) * 5,
         scratch_shapes=[
             pltpu.VMEM((4, 2, HOPS, SPAN, D), BF),
             pltpu.VMEM((7, D, SPAN), BF),
@@ -360,10 +366,14 @@
             pltpu.VMEM((SPAN, D), F32),
             pltpu.VMEM((2, YDIM, ROWS, D), BF),
             pltpu.VMEM((YDIM, ROWS, D), BF),
-            pltpu.VMEM((YDIM, ROWS, D), BF),
-            pltpu.VMEM((3, ROWS, D), BF),
-            pltpu.VMEM((XDIM, 3, 16, 384), BF),
-            pltpu.VMEM((3, 3, 16, 384), BF),
+            pltpu.VMEM((YDIM, ROWS, 384), BF),
+            pltpu.VMEM((3, ROWS, 384), BF),
+            pltpu.VMEM((XDIM, ROWS, 384), BF),
+            pltpu.VMEM((3, ROWS, 384), BF),
+            pltpu.VMEM((XDIM, 24, 384), BF),
+            pltpu.VMEM((3, 24, 384), BF),
+            pltpu.VMEM((YDIM, 24, 384), BF),
+            pltpu.VMEM((3, 24, 384), BF),
             pltpu.VMEM((GROUP, 16, 384), BF),
             pltpu.VMEM((3, 16, 384), BF),
             pltpu.VMEM((16, 384), BF),
@@ -375,18 +385,12 @@
             pltpu.VMEM((SPAN, D), BF),
             pltpu.VMEM((SPAN, D), BF),
             pltpu.VMEM((D, D), BF),
-            pltpu.VMEM((SPAN, D), BF),
-            pltpu.VMEM((SPAN, D), BF),
-            pltpu.VMEM((SPAN, D), BF),
-            pltpu.VMEM((SPAN, D), BF),
-            pltpu.VMEM((ROWS, D), F32),
-            pltpu.SemaphoreType.DMA((5,)),
             pltpu.SemaphoreType.DMA((5,)),
             pltpu.SemaphoreType.DMA((copies,)),
             pltpu.SemaphoreType.DMA((copies,)),
         ],
         compiler_params=pltpu.CompilerParams(
-            collective_id=0, has_side_effects=True, vmem_limit_bytes=67043328
+            collective_id=0, has_side_effects=True, vmem_limit_bytes=40 * 1024 * 1024
         ),
     )(partner_ids, partner_count, *flat, out_weight)
     return tuple(a.reshape(shape) for a in outs[:4]) + (outs[4],)

time: 101 us -> 106 us (1.050); the launches traced: 101 us -> 104 us
  Pallas kernels: 92.5 us -> 98.1 us
  local copies, waits for them, and re-layouts: 7.69 us -> 4.85 us
    pallas_call x1, Pallas kernels: 92.5 us -> 98.1 us  [local(): pl.pallas_call(kernel, out_shape=(rows, rows, rows, rows, jax.ShapeDtypeS...]
    unnamed x10 -> x8, local copies, waits for them, and re-layouts: 7.69 us -> 4.85 us
where the time goes in v3:
time: 106 us; the launch traced here: 104 us
  Pallas kernels  98.1 us (93%)
  local copies, waits for them, and re-layouts  4.85 us (5%)
    pallas_call x1, Pallas kernels, local(): pl.pallas_call(kernel, out_shape=(rows, rows, rows, rows, jax.ShapeDtypeS...  98.1 us
    unnamed x8, local copies, waits for them, and re-layouts  4.85 us

profile of v3, /device:TPU:24, one launch (start us, length us, event | category | flops | bytes accessed | tf_op | source)
XLA Modules:
  0.0 103.6 jit_solution(17451981629715015300)
XLA Ops:
  0.6 0.8 copy.12.ids
  1.4 0.0 copy-start
  1.4 0.7 copy-done
  2.1 98.1 %shard_map.110 = (bf16[128,768]{1,0:T(8,128)(2,1)S(1)}, bf16[128,768]{1,0:T(8,128)(2,1)S(1)}, bf16[128,768]{1,0:T(8,128)(2,1)S(1)}, bf16[128,768]{1,0:T(8,128)(2,1)S(1)}, f32[96,768]{1,0:T(8,128)S(1)}) custom-call(s32[64,6]{1,0:T(8,128)S(1)} %copy.12.ids, s32[64]{0:T(128)S(1)} %copy-done, bf16[128,768]{1,0:T(8,128)(2,1)} %bitcast.12, ...), custom_call_target="tpu_custom_call" | custom-call | tf_op jit(solution)/shard_map/pallas_call | solution.py:350
  100.2 0.7 copy.18
  100.8 0.7 copy.19
  101.5 0.7 copy.20
  102.2 0.7 copy.21
  102.9 0.7 copy.22
Async XLA Ops:
  1.4 0.7 copy-start

commit v4 on v2

--- a/solution.py
+++ b/solution.py
@@ -33,11 +33,11 @@
 
 def kernel(
     ids, cnt, q_in, k_in, v_in, g_in, w_in,
-    lo_out, dq_out, dk_out, dv_out, gw_out,
+    lo_ref, dq_ref, dk_ref, dv_ref, gw_ref,
     gat, kt, vt, s_buf, bdq, bdm, mixed_t, dq_t, stat, acc_k, acc_v,
-    gwp, w1r, w2s, w2r, xs, xr, z1s, z1r, z2s, z2r, fin, xfin,
+    gwp, w1r, ys, yr, ps, pr, z2s, z2r, fin, xfin,
     q_ref, k_ref, v_ref, g_ref, w_ref,
-    lo_ref, dq_ref, dk_ref, dv_ref, gw_ref, load, put, send, recv,
+    load, send, recv,
 ):
     loads = [
         pltpu.make_async_copy(src, dst, load.at[n])
@@ -58,11 +58,13 @@
 
     core_peer = (y * 2 + (1 - core), me)
     y_peers = [(lax.rem(y + o, YDIM) * 2 + core, me) for o in (1, 2, 3)]
-    x_peers = [(dp, lax.rem(x + o, XDIM) * ZDIM + z) for o in (1, 2, 3)]
-    zb_peers = [(dp, x * ZDIM + za * GROUP + lax.rem(zb + o, GROUP)) for o in (1, 2, 3)]
+    block_peers = [
+        (dp, lax.rem(x + o // GROUP, XDIM) * ZDIM + za * GROUP + lax.rem(zb + o % GROUP, GROUP))
+        for o in range(1, XDIM * GROUP)
+    ]
     za_peers = [(dp, x * ZDIM + lax.rem(za + o, GROUP) * GROUP + zb) for o in (1, 2, 3)]
     near = [station(o) for o in (1, 2, 3, -1, -2, -3)]
-    greet = [core_peer] + y_peers + x_peers + zb_peers + za_peers + near
+    greet = [core_peer] + y_peers + block_peers + za_peers + near
     barrier = pltpu.get_barrier_semaphore()
     for peer in greet:
         pl.semaphore_signal(barrier, inc=1, device_id=peer, device_id_type=MESH)
@@ -82,12 +84,6 @@
     source = (k_in, v_in, g_in, q_in)
     own = (k_ref, v_ref, g_ref, q_ref)
     flights = {}
-    puts = []
-
-    def store(n, src, dst):
-        copy = pltpu.make_async_copy(src, dst, put.at[n])
-        copy.start()
-        puts.append(copy)
 
     def hop(item, h):
         for way in (0, 1):
@@ -213,18 +209,16 @@
     arrived(QUERY, 1)
     hop(QUERY, 2)
     lo_ref[...] = dot(mixed_t[...].T, w_ref[...]).astype(BF)
-    store(0, lo_ref, lo_out)
 
     core_copy.wait_recv()
     for n in range(YDIM):
-        w2s[n] = (gwp[core, n].astype(F32) + w1r[n].astype(F32)).astype(BF)
+        ys[n] = (gwp[core, n].astype(F32) + w1r[n].astype(F32)).astype(BF)
     y_copies = [
-        remote(w2s.at[lax.rem(y + o, YDIM)], w2r.at[o - 1], 31 + o - 1, y_peers[o - 1])
+        remote(ys.at[lax.rem(y + o, YDIM)], yr.at[o - 1], 31 + o - 1, y_peers[o - 1])
         for o in (1, 2, 3)
     ]
 
     dq_ref[...] = dq_t[...].T
-    store(1, dq_ref, dq_out)
     acc_k[...] = jnp.zeros_like(acc_k)
     acc_v[...] = jnp.zeros_like(acc_v)
 
@@ -256,43 +250,35 @@
 
     for copy in y_copies:
         copy.wait_recv()
-    total = w2s[y].astype(F32)
+    total = ys[y].astype(F32)
     for n in range(3):
-        total = total + w2r[n].astype(F32)
+        total = total + yr[n].astype(F32)
     for n in range(XDIM):
         for r in range(3):
             lower = n * 24 + r * 8
             piece = total[lower : lower + 8]
-            xs[n, r] = jnp.concatenate([piece[:, 0:384], piece[:, 384:768]], 0).astype(BF)
-    x_copies = [
-        remote(xs.at[lax.rem(x + o, XDIM)], xr.at[o - 1], 34 + o - 1, x_peers[o - 1])
-        for o in (1, 2, 3)
+            ps[n, r] = jnp.concatenate([piece[:, 0:384], piece[:, 384:768]], 0).astype(BF)
+        ps[n, 3] = jnp.zeros((16, 384), BF)
+    block_copies = [
+        remote(
+            ps.at[lax.rem(x + o // GROUP, XDIM), lax.rem(zb + o % GROUP, GROUP)],
+            pr.at[o - 1], 34 + o - 1, block_peers[o - 1],
+        )
+        for o in range(1, XDIM * GROUP)
     ]
     prepare(2, 1)
     backward(2, 1)
 
-    for copy in x_copies:
-        copy.wait_recv()
-    part = xs[x].astype(F32)
-    for n in range(3):
-        part = part + xr[n].astype(F32)
-    z1s[0:3] = part.astype(BF)
-    z1s[3] = jnp.zeros_like(z1s[3])
-    zb_copies = [
-        remote(z1s.at[lax.rem(zb + o, GROUP)], z1r.at[o - 1], 37 + o - 1, zb_peers[o - 1])
-        for o in (1, 2, 3)
-    ]
+    for copy in block_copies:
+        copy.wait_recv()
+    part = ps[x, zb].astype(F32)
+    for n in range(XDIM * GROUP - 1):
+        part = part + pr[n].astype(F32)
+    z2s[...] = part.astype(BF)
+    za_copies = [remote(z2s, z2r.at[o - 1], 64 + o - 1, za_peers[o - 1]) for o in (1, 2, 3)]
+
     prepare(5, 0)
     backward(5, 0)
-
-    for copy in zb_copies:
-        copy.wait_recv()
-    part = z1s[zb].astype(F32)
-    for n in range(3):
-        part = part + z1r[n].astype(F32)
-    z2s[...] = part.astype(BF)
-    za_copies = [remote(z2s, z2r.at[o - 1], 40 + o - 1, za_peers[o - 1]) for o in (1, 2, 3)]
-
     arrived(GRAD, 3)
     arrived(QUERY, 3)
     prepare(3, 1)
@@ -301,23 +287,19 @@
     backward(6, 0)
     dk_ref[...] = acc_k[...].astype(BF)
     dv_ref[...] = acc_v[...].astype(BF)
-    store(2, dk_ref, dk_out)
-    store(3, dv_ref, dv_out)
 
     for copy in za_copies:
         copy.wait_recv()
     part = z2s[...].astype(F32)
     for n in range(3):
         part = part + z2r[n].astype(F32)
-    fin[zb] = (part * (1.0 / math.sqrt(DP * STATIONS * SPAN))).astype(BF)
-    zb_copies = [remote(fin.at[zb], fin.at[zb], 43 + o - 1, zb_peers[o - 1]) for o in (1, 2, 3)]
-    for copy in zb_copies:
-        copy.wait_recv()
-    x_copies = [
-        remote(fin.at[pl.ds(0, 3)], xfin.at[x], 46 + o - 1, x_peers[o - 1]) for o in (1, 2, 3)
-    ]
-    xfin[x] = fin[0:3]
-    for copy in x_copies:
+    fin[...] = (part * (1.0 / math.sqrt(DP * STATIONS * SPAN))).astype(BF)
+    block_copies = [
+        remote(fin, xfin.at[x, zb], 49 + o - 1, block_peers[o - 1])
+        for o in range(1, XDIM * GROUP)
+    ]
+    xfin[x, zb] = fin[...]
+    for copy in block_copies:
         copy.wait_recv()
     for n in range(XDIM):
         for r in range(3):
@@ -325,27 +307,29 @@
             piece = xfin[n, r].astype(F32)
             gw_ref[lower : lower + 8, 0:384] = piece[0:8]
             gw_ref[lower : lower + 8, 384:768] = piece[8:16]
-    store(4, gw_ref, gw_out)
     for copy in started:
         copy.wait_send()
-    for copy in puts:
-        copy.wait()
 
 
 def local(
     query_states, key_states, value_states, grad_output, out_weight, partner_ids, partner_count
 ):
     shape = query_states.shape
-    flat = [a.reshape(SPAN, D) for a in (query_states, key_states, value_states, grad_output)]
-    hbm = pl.BlockSpec(memory_space=pl.ANY)
+    flat = [
+        pltpu.with_memory_space_constraint(a.reshape(SPAN, D), pltpu.HBM)
+        for a in (query_states, key_states, value_states, grad_output)
+    ]
+    out_weight = pltpu.with_memory_space_constraint(out_weight, pltpu.HBM)
+    hbm = pl.BlockSpec(memory_space=pltpu.HBM)
+    vmem = pl.BlockSpec(memory_space=pltpu.VMEM)
     smem = pl.BlockSpec(memory_space=pltpu.SMEM)
     rows = jax.ShapeDtypeStruct((SPAN, D), BF)
-    copies = 49
+    copies = 67
     outs = pl.pallas_call(
         kernel,
         out_shape=(rows, rows, rows, rows, jax.ShapeDtypeStruct((ROWS, D), F32)),
         in_specs=[smem, smem] + [hbm] * 5,
-        out_specs=(hbm,) * 5,
+        out_specs=(vmem,) * 5,
         scratch_shapes=[
             pltpu.VMEM((4, 2, HOPS, SPAN, D), BF),
             pltpu.VMEM((7, D, SPAN), BF),
@@ -362,31 +346,23 @@
             pltpu.VMEM((YDIM, ROWS, D), BF),
             pltpu.VMEM((YDIM, ROWS, D), BF),
             pltpu.VMEM((3, ROWS, D), BF),
-            pltpu.VMEM((XDIM, 3, 16, 384), BF),
-            pltpu.VMEM((3, 3, 16, 384), BF),
-            pltpu.VMEM((GROUP, 16, 384), BF),
+            pltpu.VMEM((XDIM, GROUP, 16, 384), BF),
+            pltpu.VMEM((XDIM * GROUP - 1, 16, 384), BF),
+            pltpu.VMEM((16, 384), BF),
             pltpu.VMEM((3, 16, 384), BF),
             pltpu.VMEM((16, 384), BF),
-            pltpu.VMEM((3, 16, 384), BF),
-            pltpu.VMEM((GROUP, 16, 384), BF),
-            pltpu.VMEM((XDIM, 3, 16, 384), BF),
+            pltpu.VMEM((XDIM, GROUP, 16, 384), BF),
             pltpu.VMEM((SPAN, D), BF),
             pltpu.VMEM((SPAN, D), BF),
             pltpu.VMEM((SPAN, D), BF),
             pltpu.VMEM((SPAN, D), BF),
             pltpu.VMEM((D, D), BF),
-            pltpu.VMEM((SPAN, D), BF),
-            pltpu.VMEM((SPAN, D), BF),
-            pltpu.VMEM((SPAN, D), BF),
-            pltpu.VMEM((SPAN, D), BF),
-            pltpu.VMEM((ROWS, D), F32),
-            pltpu.SemaphoreType.DMA((5,)),
             pltpu.SemaphoreType.DMA((5,)),
             pltpu.SemaphoreType.DMA((copies,)),
             pltpu.SemaphoreType.DMA((copies,)),
         ],
         compiler_params=pltpu.CompilerParams(
-            collective_id=0, has_side_effects=True, vmem_limit_bytes=67043328
+            collective_id=0, has_side_effects=True, vmem_limit_bytes=40 * 1024 * 1024
         ),
     )(partner_ids, partner_count, *flat, out_weight)
     return tuple(a.reshape(shape) for a in outs[:4]) + (outs[4],)

time: 101 us -> 96.4 us (0.954)
  local copies, waits for them, and re-layouts: 7.69 us -> 4.85 us
  Pallas kernels: 92.5 us -> 90.7 us
    unnamed x10 -> x8, local copies, waits for them, and re-layouts: 7.69 us -> 4.85 us
    pallas_call x1, Pallas kernels: 92.5 us -> 90.7 us  [local(): pl.pallas_call(kernel, out_shape=(rows, rows, rows, rows, jax.ShapeDtypeS...]
where the time goes in v4:
time: 96.4 us; the launch traced here: 96.2 us
  Pallas kernels  90.7 us (94%)
  local copies, waits for them, and re-layouts  4.85 us (5%)
    pallas_call x1, Pallas kernels, local(): pl.pallas_call(kernel, out_shape=(rows, rows, rows, rows, jax.ShapeDtypeS...  90.7 us
    unnamed x8, local copies, waits for them, and re-layouts  4.85 us

profile of v4, /device:TPU:24, one launch (start us, length us, event | category | flops | bytes accessed | tf_op | source)
XLA Modules:
  0.0 96.2 jit_solution(1243103124096424815)
XLA Ops:
  0.6 0.8 copy.12.ids
  1.4 0.0 copy-start
  1.4 0.7 copy-done
  2.1 90.7 %shard_map.110 = (bf16[128,768]{1,0:T(8,128)(2,1)S(1)}, bf16[128,768]{1,0:T(8,128)(2,1)S(1)}, bf16[128,768]{1,0:T(8,128)(2,1)S(1)}, bf16[128,768]{1,0:T(8,128)(2,1)S(1)}, f32[96,768]{1,0:T(8,128)S(1)}) custom-call(s32[64,6]{1,0:T(8,128)S(1)} %copy.12.ids, s32[64]{0:T(128)S(1)} %copy-done, bf16[128,768]{1,0:T(8,128)(2,1)} %bitcast.12, ...), custom_call_target="tpu_custom_call" | custom-call | tf_op jit(solution)/shard_map/pallas_call | solution.py:328
  92.8 0.7 copy.18
  93.5 0.7 copy.19
  94.2 0.7 copy.20
  94.8 0.7 copy.21
  95.5 0.7 copy.22
Async XLA Ops:
  1.4 0.7 copy-start

commit v5 on v4

--- a/solution.py
+++ b/solution.py
@@ -34,7 +34,7 @@
 def kernel(
     ids, cnt, q_in, k_in, v_in, g_in, w_in,
     lo_ref, dq_ref, dk_ref, dv_ref, gw_ref,
-    gat, kt, vt, s_buf, bdq, bdm, mixed_t, dq_t, stat, acc_k, acc_v,
+    gat, kt, vt, s_buf, out_buf, bdq, bdm, mixed_t, dq_t, stat, acc_k, acc_v,
     gwp, w1r, ys, yr, ps, pr, z2s, z2r, fin, xfin,
     q_ref, k_ref, v_ref, g_ref, w_ref,
     load, send, recv,
@@ -137,9 +137,12 @@
             bdm[slot, p, 0:64, 0:128] = m_t[a : a + 64]
             bdm[slot, p, 64:128, 128:256] = m_t[b : b + 64]
 
+    def flip(item, turned, j):
+        turned[j] = block(item, j)[...].T
+
     def turn(j):
-        kt[j] = block(KEY, j)[...].T
-        vt[j] = block(VALUE, j)[...].T
+        flip(KEY, kt, j)
+        flip(VALUE, vt, j)
 
     prepare(0, 0)
     turn(0)
@@ -154,39 +157,45 @@
         turn(3 + h)
     arrived(KEY, 3)
     arrived(VALUE, 3)
-    turn(3)
-    turn(6)
+    flip(VALUE, vt, 3)
+    flip(VALUE, vt, 6)
 
     def forward(p, carry):
         cols = pl.ds(pl.multiple_of(p * 128, 128), 128)
-        rhs_q, rhs_m = bdq[0, p], bdm[0, p]
+        rhs_q = bdq[0, p]
         top = None
         for j in range(7):
             s = dot(block(KEY, j)[:, cols], rhs_q) + bias_f[j]
-            s_buf[j] = s
+            s_buf[p, j] = s
             m = jnp.max(s, 0, keepdims=True)
             top = m if top is None else jnp.maximum(top, m)
         total = jnp.zeros_like(top)
         for j in range(7):
-            e = jnp.exp(s_buf[j] - top)
-            s_buf[j] = e
+            e = jnp.exp(s_buf[p, j] - top)
+            s_buf[p, j] = e
             total = total + jnp.sum(e, 0, keepdims=True)
         inv = 1.0 / total
         out = jnp.zeros((128, 256), F32)
         for j in range(7):
-            prob = s_buf[j] * inv
-            s_buf[j] = prob
+            prob = s_buf[p, j] * inv
+            s_buf[p, j] = prob
             out = out + dot(vt[j, cols, :], prob.astype(BF))
         out = out.astype(BF)
+        out_buf[p] = out
         mixed_t[pl.ds(pl.multiple_of(p * 128, 128), 64), :] = out[0:64, 0:128]
         mixed_t[pl.ds(pl.multiple_of(p * 128 + 64, 64), 64), :] = out[64:128, 128:256]
-        delta = jnp.sum(rhs_m.astype(F32) * out.astype(F32), 0, keepdims=True)
         stat[0, pl.ds(p, 1), :] = top + jnp.log(total)
+        return carry
+
+    def query_side(p, carry):
+        cols = pl.ds(pl.multiple_of(p * 128, 128), 128)
+        rhs_m = bdm[0, p]
+        delta = jnp.sum(rhs_m.astype(F32) * out_buf[p].astype(F32), 0, keepdims=True)
         stat[0, pl.ds(p + 8, 1), :] = delta
         grad = jnp.zeros((128, 256), F32)
         for j in range(7):
             d_prob = dot(block(VALUE, j)[:, cols], rhs_m)
-            d_score = (s_buf[j] * (d_prob - delta)).astype(BF)
+            d_score = (s_buf[p, j] * (d_prob - delta)).astype(BF)
             grad = grad + dot(kt[j, cols, :], d_score)
         grad = (grad * 0.125).astype(BF)
         dq_t[pl.ds(pl.multiple_of(p * 128, 128), 64), :] = grad[0:64, 0:128]
@@ -202,14 +211,15 @@
         rows = mixed_t[d * ROWS : (d + 1) * ROWS, :]
         gwp[d % 2, d // 2] = dot(rows, g_ref[...]).astype(BF)
     core_copy = remote(gwp.at[1 - core], w1r, 30, core_peer)
+    arrived(QUERY, 1)
+    hop(QUERY, 2)
+    flip(KEY, kt, 3)
+    flip(KEY, kt, 6)
+    lax.fori_loop(0, PAIRS, query_side, 0)
     stats = []
     for d in (1, 2, 3):
         stats.append(remote(stat.at[0], stat.at[d], 24 + d - 1, station(d)))
         stats.append(remote(stat.at[0], stat.at[3 + d], 27 + d - 1, station(-d)))
-    arrived(QUERY, 1)
-    hop(QUERY, 2)
-    lo_ref[...] = dot(mixed_t[...].T, w_ref[...]).astype(BF)
-
     core_copy.wait_recv()
     for n in range(YDIM):
         ys[n] = (gwp[core, n].astype(F32) + w1r[n].astype(F32)).astype(BF)
@@ -218,6 +228,7 @@
         for o in (1, 2, 3)
     ]
 
+    lo_ref[...] = dot(mixed_t[...].T, w_ref[...]).astype(BF)
     dq_ref[...] = dq_t[...].T
     acc_k[...] = jnp.zeros_like(acc_k)
     acc_v[...] = jnp.zeros_like(acc_v)
@@ -247,6 +258,8 @@
     hop(QUERY, 3)
     prepare(4, 0)
     backward(4, 0)
+    prepare(2, 1)
+    backward(2, 1)
 
     for copy in y_copies:
         copy.wait_recv()
@@ -266,8 +279,8 @@
         )
         for o in range(1, XDIM * GROUP)
     ]
-    prepare(2, 1)
-    backward(2, 1)
+    prepare(5, 0)
+    backward(5, 0)
 
     for copy in block_copies:
         copy.wait_recv()
@@ -277,16 +290,10 @@
     z2s[...] = part.astype(BF)
     za_copies = [remote(z2s, z2r.at[o - 1], 64 + o - 1, za_peers[o - 1]) for o in (1, 2, 3)]
 
-    prepare(5, 0)
-    backward(5, 0)
     arrived(GRAD, 3)
     arrived(QUERY, 3)
     prepare(3, 1)
     backward(3, 1)
-    prepare(6, 0)
-    backward(6, 0)
-    dk_ref[...] = acc_k[...].astype(BF)
-    dv_ref[...] = acc_v[...].astype(BF)
 
     for copy in za_copies:
         copy.wait_recv()
@@ -299,6 +306,10 @@
         for o in range(1, XDIM * GROUP)
     ]
     xfin[x, zb] = fin[...]
+    prepare(6, 0)
+    backward(6, 0)
+    dk_ref[...] = acc_k[...].astype(BF)
+    dv_ref[...] = acc_v[...].astype(BF)
     for copy in block_copies:
         copy.wait_recv()
     for n in range(XDIM):
@@ -334,7 +345,8 @@
             pltpu.VMEM((4, 2, HOPS, SPAN, D), BF),
             pltpu.VMEM((7, D, SPAN), BF),
             pltpu.VMEM((7, D, SPAN), BF),
-            pltpu.VMEM((7, SPAN, 256), F32),
+            pltpu.VMEM((PAIRS, 7, SPAN, 256), F32),
+            pltpu.VMEM((PAIRS, 128, 256), BF),
             pltpu.VMEM((2, PAIRS, 128, 256), BF),
             pltpu.VMEM((2, PAIRS, 128, 256), BF),
             pltpu.VMEM((D, SPAN), BF),

time: 96.4 us -> 97.7 us (1.013)
  Pallas kernels: 90.7 us -> 92.1 us
    pallas_call x1, Pallas kernels: 90.7 us -> 92.1 us  [local(): pl.pallas_call(kernel, out_shape=(rows, rows, rows, rows, jax.ShapeDtypeS...]
where the time goes in v5:
time: 97.7 us; the launch traced here: 97.6 us
  Pallas kernels  92.1 us (94%)
  local copies, waits for them, and re-layouts  4.85 us (5%)
    pallas_call x1, Pallas kernels, local(): pl.pallas_call(kernel, out_shape=(rows, rows, rows, rows, jax.ShapeDtypeS...  92.1 us
    unnamed x8, local copies, waits for them, and re-layouts  4.85 us

profile of v5, /device:TPU:24, one launch (start us, length us, event | category | flops | bytes accessed | tf_op | source)
XLA Modules:
  0.0 97.6 jit_solution(12596410054959275726)
XLA Ops:
  0.6 0.8 copy.12.ids
  1.4 0.0 copy-start
  1.4 0.7 copy-done
  2.1 92.1 %shard_map.110 = (bf16[128,768]{1,0:T(8,128)(2,1)S(1)}, bf16[128,768]{1,0:T(8,128)(2,1)S(1)}, bf16[128,768]{1,0:T(8,128)(2,1)S(1)}, bf16[128,768]{1,0:T(8,128)(2,1)S(1)}, f32[96,768]{1,0:T(8,128)S(1)}) custom-call(s32[64,6]{1,0:T(8,128)S(1)} %copy.12.ids, s32[64]{0:T(128)S(1)} %copy-done, bf16[128,768]{1,0:T(8,128)(2,1)} %bitcast.12, ...), custom_call_target="tpu_custom_call" | custom-call | tf_op jit(solution)/shard_map/pallas_call | solution.py:339
  94.2 0.7 copy.18
  94.8 0.7 copy.19
  95.5 0.7 copy.20
  96.2 0.7 copy.21
  96.9 0.7 copy.22
Async XLA Ops:
  1.4 0.7 copy-start
